TPU v7x, 32 devices: a whole 2x2x4 slice. The times are simulated.
32 devices in a mesh: fsdp: 4 (over z), ctx: 4 (over x, core), tp: 2 (over y).
Axes of the slice: x: 2, y: 2, z: 4, core: 2. Of those that a mesh axis runs over, the one named last changes fastest.
Arguments:
- x_in: bfloat16 [8, 1024, 2048], P(None, ('fsdp', 'ctx')), may hold values from -6 to 6
- cotangent: bfloat16 [8, 1024, 2048], P(None, ('fsdp', 'ctx')), may hold values from -6 to 6
- lengths: int32 [8], replicated, may hold values from 128 to 1024, as said below
- adapter_ids: int32 [8], replicated, may hold values from 0 to 7
- w_qkv: bfloat16 [3, 2048, 2048], P(None, 'fsdp', 'tp'), may hold values from -0.125 to 0.125
- w_out: bfloat16 [2048, 2048], P('tp', 'fsdp'), may hold values from -2 to 2
- w_up: bfloat16 [2048, 8192], P('fsdp', 'tp'), may hold values from -0.125 to 0.125
- w_down: bfloat16 [8192, 2048], P('tp', 'fsdp'), may hold values from -0.0625 to 0.0625
- ln_gain: float32 [2, 2048], replicated, may hold values from 0.1 to 1.9
- ln_bias: float32 [2, 2048], replicated, may hold values from -1.5 to 1.5
- a_qkv: bfloat16 [3, 2048, 128], replicated, may hold values from -0.125 to 0.125
- b_qkv: bfloat16 [3, 128, 2048], P(None, None, 'tp'), may hold values from -0.5 to 0.5
- a_out: bfloat16 [2048, 128], P('tp'), may hold values from -2 to 2
- b_out: bfloat16 [128, 2048], replicated, may hold values from -0.5 to 0.5
- a_up: bfloat16 [2048, 128], replicated, may hold values from -0.125 to 0.125
- b_up: bfloat16 [128, 8192], P(None, 'tp'), may hold values from -0.5 to 0.5
- a_down: bfloat16 [8192, 128], P('tp'), may hold values from -0.0625 to 0.0625
- b_down: bfloat16 [128, 2048], replicated, may hold values from -0.5 to 0.5
Outputs:
- activations: bfloat16 [8, 1024, 2048], P(None, ('fsdp', 'ctx'))
- input_grad: bfloat16 [8, 1024, 2048], P(None, ('fsdp', 'ctx'))
- grad_a_qkv: float32 [3, 2048, 128], replicated
- grad_b_qkv: float32 [3, 128, 2048], P(None, None, 'tp')
- grad_a_out: float32 [2048, 128], P('tp')
- grad_b_out: float32 [128, 2048], replicated
- grad_a_up: float32 [2048, 128], replicated
- grad_b_up: float32 [128, 8192], P(None, 'tp')
- grad_a_down: float32 [8192, 128], P('tp')
- grad_b_down: float32 [128, 2048], replicated
Inputs may be any that keep to these rules, and one draw needn't show every extreme that they name: `lengths`: each aligned block of 2 sequences holds at least one sequence of length 1024.
All inputs are finite; a program needn't handle non-finite values.
Results may differ from a plain program's by a relative error of at most 0.019.
Values may be sent and summed in bfloat16 or wider, within the bound.
A program may use at most 256 MiB of HBM per device.

v0:
```python
from functools import partial
import math
import jax
import jax.numpy as jnp
from jax import lax
from jax.sharding import PartitionSpec as P

HEAD_DIM = 128
RANK = 16
ADAPTERS = 8
NORM_EPS = 1e-06
GELU_COEF = 0.7978845608028654


def norm_rows(values, gain_row, shift_row):
    center = values - jnp.mean(values, axis=-1, keepdims=True)
    spread = jnp.mean(center * center, axis=-1, keepdims=True)
    return center * lax.rsqrt(spread + NORM_EPS) * gain_row + shift_row


def gelu_tanh(values):
    return (
        0.5 * values * (1.0 + jnp.tanh(GELU_COEF * (values + 0.044715 * values * values * values)))
    )


def product(left_side, right_side):
    return jnp.dot(left_side, right_side, preferred_element_type=jnp.float32)


def against(left_side, right_side):
    return lax.dot_general(
        left_side, right_side, (((1,), (1,)), ((), ())), preferred_element_type=jnp.float32
    )


def across(left_side, right_side):
    return lax.dot_general(
        left_side, right_side, (((0,), (0,)), ((), ())), preferred_element_type=jnp.float32
    )


def local(
    x_in,
    cotangent,
    lengths,
    adapter_ids,
    w_qkv,
    w_out,
    w_up,
    w_down,
    ln_gain,
    ln_bias,
    a_qkv,
    b_qkv,
    a_out,
    b_out,
    a_up,
    b_up,
    a_down,
    b_down,
):
    n_ctx = lax.axis_size("ctx")
    n_fsdp = lax.axis_size("fsdp")
    owner_index = lax.axis_index("fsdp")
    seq_total, piece_rows, model_width = x_in.shape
    per_dev = seq_total // n_fsdp
    local_len = n_fsdp * piece_rows
    dev_rows = per_dev * local_len
    key_count = n_ctx * local_len
    heads_width = w_qkv.shape[2]
    heads_here = heads_width // HEAD_DIM
    score_scale = 1.0 / math.sqrt(HEAD_DIM)
    dealt_x, dealt_cot = (
        lax.all_to_all(x_in, "fsdp", split_axis=0, concat_axis=1, tiled=True),
        lax.all_to_all(cotangent, "fsdp", split_axis=0, concat_axis=1, tiled=True),
    )
    x_rows = dealt_x.reshape(dev_rows, model_width)
    my_lengths = lax.dynamic_slice_in_dim(lengths, owner_index * per_dev, per_dev)
    my_ids = lax.dynamic_slice_in_dim(adapter_ids, owner_index * per_dev, per_dev)
    picked = (my_ids[:, None] == jnp.arange(ADAPTERS)[None, :]).astype(jnp.float32)
    pick_rows = jnp.repeat(jnp.repeat(picked, RANK, axis=1), local_len, axis=0)
    key_index = jnp.arange(key_count)
    ctx_block = key_index // local_len
    remain = key_index % local_len
    key_pos = (remain // piece_rows * n_ctx + ctx_block) * piece_rows + remain % piece_rows
    usable = key_pos[None, :] < my_lengths[:, None]
    qkv_full, out_full = (
        lax.all_gather(w_qkv, "fsdp", axis=1, tiled=True),
        lax.all_gather(w_out, "fsdp", axis=1, tiled=True),
    )
    adapt_qkv = [
        (product(x_rows, a_qkv[proj_index]) * pick_rows).astype(jnp.bfloat16)
        for proj_index in range(3)
    ]
    projected = [
        (product(x_rows, qkv_full[proj_index]) + product(adapt_qkv[proj_index], b_qkv[proj_index]))
        .astype(jnp.bfloat16)
        .reshape(per_dev, local_len, heads_width)
        for proj_index in range(3)
    ]
    queries_all = projected[0]
    keys_all, values_all = (
        lax.all_gather(projected[1], "ctx", axis=1, tiled=True),
        lax.all_gather(projected[2], "ctx", axis=1, tiled=True),
    )

    def score_block(query_heads, key_heads, usable_row):
        scores = (
            jnp.einsum("qhd,khd->hqk", query_heads, key_heads, preferred_element_type=jnp.float32)
            * score_scale
        )
        return jnp.where(usable_row[None, None, :], scores, -1e30)

    def attend(packed):
        queries, keys_seq, values_seq, usable_row = packed
        query_heads = queries.reshape(local_len, heads_here, HEAD_DIM)
        key_heads = keys_seq.reshape(key_count, heads_here, HEAD_DIM)
        value_heads = values_seq.reshape(key_count, heads_here, HEAD_DIM)
        scores = score_block(query_heads, key_heads, usable_row)
        row_max = jnp.max(scores, axis=-1, keepdims=True)
        row_total = jnp.sum(jnp.exp(scores - row_max), axis=-1, keepdims=True)
        log_total = row_max + jnp.log(row_total)
        attn_probs = jnp.exp(scores - log_total).astype(jnp.bfloat16)
        mixed_heads = jnp.einsum(
            "hqk,khd->qhd", attn_probs, value_heads, preferred_element_type=jnp.float32
        )
        return (mixed_heads.reshape(local_len, heads_width).astype(jnp.bfloat16), log_total[..., 0])

    context, log_totals = lax.map(attend, (queries_all, keys_all, values_all, usable))
    ctx_rows = context.reshape(dev_rows, heads_width)
    part_out = product(ctx_rows, out_full)
    part_adapt = product(ctx_rows, a_out) * pick_rows
    attn_sum, adapt_out_sum = lax.psum((part_out, part_adapt), "tp")
    adapt_out = adapt_out_sum.astype(jnp.bfloat16)
    attn_branch = attn_sum + product(adapt_out, b_out)
    hidden_one, norm_one_back = jax.vjp(
        partial(norm_rows, gain_row=ln_gain[0], shift_row=ln_bias[0]),
        x_rows.astype(jnp.float32) + attn_branch,
    )
    hidden_low = hidden_one.astype(jnp.bfloat16)
    up_full, down_full = (
        lax.all_gather(w_up, "fsdp", axis=0, tiled=True),
        lax.all_gather(w_down, "fsdp", axis=1, tiled=True),
    )
    adapt_up = (product(hidden_low, a_up) * pick_rows).astype(jnp.bfloat16)
    pre_act = product(hidden_low, up_full) + product(adapt_up, b_up)
    activated, gelu_back = jax.vjp(gelu_tanh, pre_act)
    gelu_out = activated.astype(jnp.bfloat16)
    part_down = product(gelu_out, down_full)
    part_adapt_down = product(gelu_out, a_down) * pick_rows
    down_sum, adapt_down_sum = lax.psum((part_down, part_adapt_down), "tp")
    adapt_down = adapt_down_sum.astype(jnp.bfloat16)
    second_in = hidden_one + down_sum + product(adapt_down, b_down)
    layer_out, norm_two_back = jax.vjp(
        partial(norm_rows, gain_row=ln_gain[1], shift_row=ln_bias[1]), second_in
    )
    grad_out = dealt_cot.reshape(dev_rows, model_width).astype(jnp.float32)
    (grad_second,) = norm_two_back(grad_out)
    grad_down_low = grad_second.astype(jnp.bfloat16)
    up_back, down_back = (
        lax.all_gather(w_up, "fsdp", axis=0, tiled=True),
        lax.all_gather(w_down, "fsdp", axis=1, tiled=True),
    )
    grad_adapt_down = (against(grad_down_low, b_down) * pick_rows).astype(jnp.bfloat16)
    grad_b_down = across(adapt_down, grad_down_low)
    grad_a_down = across(gelu_out, grad_adapt_down)
    grad_gelu = against(grad_down_low, down_back) + against(grad_adapt_down, a_down)
    (grad_pre,) = gelu_back(grad_gelu)
    grad_pre_low = grad_pre.astype(jnp.bfloat16)
    grad_b_up = across(adapt_up, grad_pre_low)
    part_hidden = against(grad_pre_low, up_back)
    part_adapt_up = against(grad_pre_low, b_up)
    grad_hidden_sum, grad_adapt_up_sum = lax.psum((part_hidden, part_adapt_up), "tp")
    grad_adapt_up = (grad_adapt_up_sum * pick_rows).astype(jnp.bfloat16)
    grad_a_up = across(hidden_low, grad_adapt_up)
    grad_hidden = grad_second + grad_hidden_sum + against(grad_adapt_up, a_up)
    (grad_first,) = norm_one_back(grad_hidden)
    grad_attn_low = grad_first.astype(jnp.bfloat16)
    qkv_back, out_back = (
        lax.all_gather(w_qkv, "fsdp", axis=1, tiled=True),
        lax.all_gather(w_out, "fsdp", axis=1, tiled=True),
    )
    grad_adapt_out = (against(grad_attn_low, b_out) * pick_rows).astype(jnp.bfloat16)
    grad_b_out = across(adapt_out, grad_attn_low)
    grad_a_out = across(ctx_rows, grad_adapt_out)
    grad_context = (against(grad_attn_low, out_back) + against(grad_adapt_out, a_out)).astype(
        jnp.bfloat16
    )

    def attend_back(packed):
        queries, keys_seq, values_seq, usable_row, log_total, grad_ctx_seq = packed
        query_heads = queries.reshape(local_len, heads_here, HEAD_DIM)
        key_heads = keys_seq.reshape(key_count, heads_here, HEAD_DIM)
        value_heads = values_seq.reshape(key_count, heads_here, HEAD_DIM)
        scores = score_block(query_heads, key_heads, usable_row)
        attn_probs = jnp.exp(scores - log_total[..., None])
        probs_low = attn_probs.astype(jnp.bfloat16)
        grad_heads = grad_ctx_seq.reshape(local_len, heads_here, HEAD_DIM)
        grad_values = jnp.einsum(
            "hqk,qhd->khd", probs_low, grad_heads, preferred_element_type=jnp.float32
        )
        grad_probs = jnp.einsum(
            "qhd,khd->hqk", grad_heads, value_heads, preferred_element_type=jnp.float32
        )
        row_dot = jnp.sum(attn_probs * grad_probs, axis=-1, keepdims=True)
        grad_scores = (attn_probs * (grad_probs - row_dot)).astype(jnp.bfloat16)
        grad_query = (
            jnp.einsum("hqk,khd->qhd", grad_scores, key_heads, preferred_element_type=jnp.float32)
            * score_scale
        )
        grad_keys = (
            jnp.einsum("hqk,qhd->khd", grad_scores, query_heads, preferred_element_type=jnp.float32)
            * score_scale
        )
        return (
            grad_query.reshape(local_len, heads_width).astype(jnp.bfloat16),
            grad_keys.reshape(key_count, heads_width),
            grad_values.reshape(key_count, heads_width),
        )

    grad_ctx_seqs = grad_context.reshape(per_dev, local_len, heads_width)
    grad_queries, grad_keys_all, grad_values_all = lax.map(
        attend_back, (queries_all, keys_all, values_all, usable, log_totals, grad_ctx_seqs)
    )
    grad_keys_mine, grad_values_mine = (
        lax.psum_scatter(
            grad_keys_all.astype(jnp.bfloat16), "ctx", scatter_dimension=1, tiled=True
        ).astype(jnp.float32),
        lax.psum_scatter(
            grad_values_all.astype(jnp.bfloat16), "ctx", scatter_dimension=1, tiled=True
        ).astype(jnp.float32),
    )
    grad_proj = [
        grad_queries.reshape(dev_rows, heads_width),
        grad_keys_mine.astype(jnp.bfloat16).reshape(dev_rows, heads_width),
        grad_values_mine.astype(jnp.bfloat16).reshape(dev_rows, heads_width),
    ]
    grad_b_qkv = jnp.stack(
        [across(adapt_qkv[proj_index], grad_proj[proj_index]) for proj_index in range(3)]
    )
    part_input = (
        against(grad_proj[0], qkv_back[0])
        + against(grad_proj[1], qkv_back[1])
        + against(grad_proj[2], qkv_back[2])
    )
    part_adapt_qkv = jnp.stack(
        [against(grad_proj[proj_index], b_qkv[proj_index]) for proj_index in range(3)]
    )
    grad_input_sum, grad_adapt_qkv_sum = (
        lax.psum(part_input.astype(jnp.bfloat16), "tp").astype(jnp.float32),
        lax.psum(part_adapt_qkv.astype(jnp.bfloat16), "tp").astype(jnp.float32),
    )
    grad_adapt_qkv = (grad_adapt_qkv_sum * pick_rows[None]).astype(jnp.bfloat16)
    grad_a_qkv = jnp.stack([across(x_rows, grad_adapt_qkv[proj_index]) for proj_index in range(3)])
    grad_input = (
        grad_first
        + grad_input_sum
        + against(grad_adapt_qkv[0], a_qkv[0])
        + against(grad_adapt_qkv[1], a_qkv[1])
        + against(grad_adapt_qkv[2], a_qkv[2])
    )
    summed_grads = lax.psum(
        (
            grad_a_qkv,
            grad_b_qkv,
            grad_a_out,
            grad_b_out,
            grad_a_up,
            grad_b_up,
            grad_a_down,
            grad_b_down,
        ),
        ("fsdp", "ctx"),
    )
    out_low = layer_out.astype(jnp.bfloat16).reshape(per_dev, local_len, model_width)
    input_low = grad_input.astype(jnp.bfloat16).reshape(per_dev, local_len, model_width)
    back_out, back_input = (
        lax.all_to_all(out_low, "fsdp", split_axis=1, concat_axis=0, tiled=True),
        lax.all_to_all(input_low, "fsdp", split_axis=1, concat_axis=0, tiled=True),
    )
    return (
        back_out,
        back_input,
        summed_grads[0],
        summed_grads[1],
        summed_grads[2],
        summed_grads[3],
        summed_grads[4],
        summed_grads[5],
        summed_grads[6],
        summed_grads[7],
    )


def solution(mesh):
    return jax.shard_map(
        local,
        mesh=mesh,
        in_specs=(
            P(None, ("fsdp", "ctx"), None),
            P(None, ("fsdp", "ctx"), None),
            P(),
            P(),
            P(None, "fsdp", "tp"),
            P("tp", "fsdp"),
            P("fsdp", "tp"),
            P("tp", "fsdp"),
            P(),
            P(),
            P(),
            P(None, None, "tp"),
            P("tp", None),
            P(),
            P(),
            P(None, "tp"),
            P("tp", None),
            P(),
        ),
        out_specs=(
            P(None, ("fsdp", "ctx"), None),
            P(None, ("fsdp", "ctx"), None),
            P(),
            P(None, None, "tp"),
            P("tp", None),
            P(),
            P(),
            P(None, "tp"),
            P("tp", None),
            P(),
        ),
        check_vma=False,
    )
```

profile of v0, /device:TPU:0, one launch (start us, length us, event | category | flops | bytes accessed | tf_op | source)
XLA Modules:
  0.0 2011.4 jit_solution(7236679362293835580)
XLA Ops:
  7.9 6.3 all-to-all-start
  14.6 104.2 %all-to-all-done = bf16[8,64,2048]{2,1,0:T(8,128)(2,1)S(1)} async-done(((bf16[8,64,2048]{2,1,0:T(8,128)(2,1)}), bf16[8,64,2048]{2,1,0:T(8,128)(2,1)S(1)}, u32[]{:S(2)}, u32[]{:S(2)}) %all-to-all-start) | async-done | bytes 2097184 | tf_op jit(solution)/shard_map/all_to_all | solution.py:75
  124.0 141.4 %all-gather.7.cloned.1.call-done = bf16[3,2048,1024]{2,1,0:T(8,128)(2,1)} async-done(((bf16[3,512,1024]{2,1,0:T(8,128)(2,1)}), bf16[3,2048,1024]{2,1,0:T(8,128)(2,1)}) %all-gather.7.cloned.1.call-update) | async-done | bytes 12582928 | tf_op jit(solution)/shard_map/all_gather | solution.py:89
  297.6 11.3 all-gather.11.cloned.1.call-done
  308.8 37.2 %all-gather.9.cloned.1.call-done = bf16[2,1024,1024]{1,2,0:T(8,128)(2,1)} async-done(((bf16[2,256,1024]{1,2,0:T(8,128)(2,1)}), bf16[2,1024,1024]{1,2,0:T(8,128)(2,1)}) %all-gather.9.cloned.1.call-update) | async-done | bytes 4194320 | tf_op jit(solution)/shard_map/all_gather | solution.py:105
  347.1 26.9 %while.26 = (s32[]{:T(128)}, bf16[2,256,1024]{2,1,0:T(8,128)(2,1)}, f32[2,8,256]{2,1,0:T(8,128)S(1)}, bf16[2,1024,1024]{1,2,0:T(8,128)(2,1)}, pred[2,1024]{1,0:T...) while((s32[]{:T(128)}, bf16[2,256,1024]{2,1,0:T(8,128)(2,1)}, ...), condition=%wide.region_3.4_spmd, body=%wide.region_0.3_spmd.sunk | while | flops 1097070592 | bytes 46208640 | solution.py:130
  374.1 54.2 %all-gather.13.cloned.1.call-done = bf16[1024,2048]{1,0:T(8,128)(2,1)} async-done(((bf16[1024,512]{1,0:T(8,128)(2,1)}), bf16[1024,2048]{1,0:T(8,128)(2,1)}) %all-gather.13.cloned.1.call-update) | async-done | bytes 4194320 | tf_op jit(solution)/shard_map/all_gather | solution.py:90
  428.3 6.8 fusion.101
  439.0 19.6 all-reduce.20
  458.6 88.7 %all-reduce.11.cloned.1.call-done = f32[512,2048]{1,0:T(8,128)} async-done(((f32[512,2048]{1,0:T(8,128)}), f32[512,2048]{1,0:T(8,128)}) %all-reduce.11.cloned.1.call-update) | async-done | bytes 4194320 | tf_op jit(solution)/shard_map/psum | solution.py:134
  559.5 276.1 %all-gather.15.cloned.1.call-done = bf16[2048,4096]{1,0:T(8,128)(2,1)} async-done(((bf16[512,4096]{1,0:T(8,128)(2,1)}), bf16[2048,4096]{1,0:T(8,128)(2,1)}) %all-gather.15.cloned.1.call-update) | async-done | bytes 16777232 | tf_op jit(solution)/shard_map/all_gather | solution.py:143
  835.6 20.4 %multiply_convert_fusion.1 = (bf16[512,4096]{1,0:T(8,128)(2,1)}, f32[512,4096]{1,0:T(8,128)}) fusion(f32[512,4096]{1,0:T(8,128)} %fusion.102, bf16[512,2048]{1,0:T(8,128)(2,1)S(1)} %fusion.31, bf16[2048,4096]{1,0:T(8,128)(2,1)} %all-gather.15.cloned.1.call-done), kind=kOutput, calls=%fused_computation.52 | convolution fusion | flops 8610906112 | bytes 39845888 | tf_op jit(solution)/shard_map/dot_general | solution.py:28
  856.0 266.2 %all-gather.17.cloned.1.call-done = bf16[4096,2048]{1,0:T(8,128)(2,1)} async-done(((bf16[4096,512]{1,0:T(8,128)(2,1)}), bf16[4096,2048]{1,0:T(8,128)(2,1)}) %all-gather.17.cloned.1.call-update) | async-done | bytes 16777232 | tf_op jit(solution)/shard_map/all_gather | solution.py:144
  1122.2 14.9 fusion.103
  1138.7 51.1 %all_to_all.60 = bf16[8,64,2048]{2,1,0:T(8,128)(2,1)S(1)} all-to-all(bf16[8,64,2048]{2,1,0:T(8,128)(2,1)S(1)} %copy-done.39), channel_id=1, replica_groups=mesh['fsdp'=4,'ctx'=4,'tp'=2] {'fsdp'}, dimensions={0} | all-to-all | bytes 4194304 | tf_op jit(solution)/shard_map/all_to_all | solution.py:76
  1194.8 18.6 all-reduce.21
  1213.4 35.5 %all-reduce.13.cloned.1.call-done = f32[512,2048]{1,0:T(8,128)} async-done(((f32[512,2048]{1,0:T(8,128)}), f32[512,2048]{1,0:T(8,128)}) %all-reduce.13.cloned.1.call-update) | async-done | bytes 4194320 | tf_op jit(solution)/shard_map/psum | solution.py:152
  1264.7 22.3 %fusion.22 = bf16[512,4096]{1,0:T(8,128)(2,1)} fusion(f32[512,4096]{1,0:T(8,128)} %get-tuple-element.250, f32[512,4096]{1,0:T(8,128)} %fusion.104, bf16[512,2048]{1,0:T(8,128)(2,1)S(1)} %add_convert_fusion.4, bf16[4096,2048]{1,0:T(8,128)(2,1)} %all-gather.17.cloned.1.call-done), kind=kOutput, calls=%fused_computation.49 | convolution fusion | flops 8642363392 | bytes 39845888 | tf_op jit(solution)/shard_map/dot_general | solution.py:32
  1291.3 14.0 fusion.105
  1305.4 113.3 %all-reduce.17.cloned.1.call-done = (f32[512,2048]{1,0:T(8,128)}, f32[512,128]{1,0:T(8,128)}) async-done(((f32[512,2048]{1,0:T(8,128)}, f32[512,128]{1,0:T(8,128)}), (f32[512,2048]{1,0:T(8,128)}, f32[512,128]{1,0:T(8,128)})) %all-reduce.17.cloned.1.call-update) | async-done | bytes 4456464 | tf_op jit(solution)/shard_map/psum | solution.py:174
  1419.7 6.1 multiply_reduce_fusion.1
  1436.4 91.7 %while.27 = (s32[]{:T(128)}, bf16[2,256,1024]{2,1,0:T(8,128)(2,1)}, bf16[2,1024,1024]{2,1,0:T(8,128)(2,1)}, bf16[2,1024,1024]{2,1,0:T(8,128)(2,1)}, bf16[2,1024,...) while((s32[]{:T(128)}, bf16[2,256,1024]{2,1,0:T(8,128)(2,1)}, ...), condition=%wide.region_20.21_spmd, body=%wide.region_18.20_spmd.sunk | while | flops 2718431232 | bytes 173603120 | solution.py:223
  1447.1 6.4 multiply_reduce_fusion.6
  1464.0 6.8 fusion.233
  1492.8 6.4 multiply_reduce_fusion.6
  1509.7 6.8 fusion.233
  1538.7 6.8 fusion.27
  1545.5 27.2 %reduce-scatter.3.cloned.1.call-done = bf16[2,256,1024]{2,1,0:T(8,128)(2,1)} async-done(((bf16[2,1024,1024]{2,1,0:T(8,128)(2,1)}), bf16[2,256,1024]{2,1,0:T(8,128)(2,1)}) %reduce-scatter.3.cloned.1.call-update) | async-done | bytes 1048592 | tf_op jit(solution)/shard_map/reduce_scatter | solution.py:227
  1574.4 45.4 %reduce-scatter.5.cloned.1.call-done = bf16[2,256,1024]{2,1,0:T(8,128)(2,1)} async-done(((bf16[2,1024,1024]{2,1,0:T(8,128)(2,1)}), bf16[2,256,1024]{2,1,0:T(8,128)(2,1)}) %reduce-scatter.5.cloned.1.call-update) | async-done | bytes 1048592 | tf_op jit(solution)/shard_map/reduce_scatter | solution.py:230
  1649.0 56.3 %all-reduce.19.cloned.1.call-done = (bf16[3,512,128]{2,1,0:T(8,128)(2,1)}, bf16[512,2048]{1,0:T(8,128)(2,1)}) async-done(((bf16[3,512,128]{2,1,0:T(8,128)(2,1)}, bf16[512,2048]{1,0:T(8,128)(2,1)}), (bf16[3,512,128]{2,1,0:T(8,128)(2,1)}, bf16[512,2048]{1,0:T(8,128)(2,1)})) %all-reduce.19.cloned.1.call-update) | async-done | bytes 2490384 | tf_op jit(solution)/shard_map/psum | solution.py:252
  1727.2 67.8 %all-to-all-done.3 = bf16[2,256,2048]{2,0,1:T(2,128)(2,1)S(1)} async-done(((bf16[2,256,2048]{2,0,1:T(2,128)(2,1)}), bf16[2,256,2048]{2,0,1:T(2,128)(2,1)S(1)}, u32[]{:S(2)}, u32[]{:S(2)}) %all-to-all-start.3) | async-done | bytes 2097184 | tf_op jit(solution)/shard_map/all_to_all | solution.py:280
  1797.2 196.3 %all-reduce.15.cloned.1.call-done = (f32[3,2048,128]{1,2,0:T(8,128)}, f32[3,128,1024]{2,1,0:T(8,128)}, f32[1024,128]{1,0:T(8,128)}, f32[128,2048]{1,0:T(8,128)},...) async-done(((f32[3,2048,128]{1,2,0:T(8,128)}, f32[3,128,1024]{2,1,0:T(8,128)}, f32[1024,128]{1,0:T(8,128)}, ...) | async-done | bytes 12582928 | tf_op jit(solution)/shard_map/psum | solution.py:263
  (357 shorter events, 261.4 us)
Async XLA Ops:
  7.2 1185.3 %copy-start = (bf16[4096,128]{1,0:T(8,128)(2,1)S(1)}, bf16[4096,128]{1,0:T(8,128)(2,1)}, u32[]{:S(2)}) copy-start(bf16[4096,128]{1,0:T(8,128)(2,1)} %param.38) | copy-start | bytes 3145732
  7.2 7.1 copy-start.80
  7.2 258.2 %all-gather.7.cloned.1.call-start = ((), (), s32[]{:S(2)}) async-start(), calls=%async_computation.6 | async-start | bytes 15728640 | tf_op jit(solution)/shard_map/all_gather | solution.py:89
  7.9 110.8 %all-to-all-start = ((bf16[8,64,2048]{2,1,0:T(8,128)(2,1)}), bf16[8,64,2048]{2,1,0:T(8,128)(2,1)S(1)}, u32[]{:S(2)}, u32[]{:S(2)}) async-start(bf16[8,64,2048]{2,1,0:T(8,128)(2,1)} %param.22), calls=%async_computation | async-start | bytes 4194304 | tf_op jit(solution)/shard_map/all_to_all | solution.py:75
  14.3 294.6 %all-gather.11.cloned.1.call-start = ((), (), s32[]{:S(2)}) async-start(), calls=%async_computation.8 | async-start | bytes 5242880 | tf_op jit(solution)/shard_map/all_gather | solution.py:104
  14.6 1413.2 %copy-start.71 = (f32[2,128]{1,0:T(2,128)}, f32[2,128]{1,0:T(2,128)S(1)}, u32[]{:S(2)}) copy-start(f32[2,128]{1,0:T(2,128)S(1)} %reshape.257) | copy-start | bytes 3076
  121.8 425.5 %copy-start.6 = (bf16[4,2,64,2048]{3,2,0,1:T(8,128)(2,1)}, bf16[4,2,64,2048]{3,2,0,1:T(8,128)(2,1)S(1)}, u32[]{:S(2)}) copy-start(bf16[4,2,64,2048]{3,2,0,1:T(8,128)(2,1)S(1)} %copy.63) | copy-start | bytes 6291460
  124.0 145.9 %copy-start.53 = (bf16[512,128]{1,0:T(8,128)(2,1)}, bf16[512,128]{1,0:T(8,128)(2,1)S(1)}, u32[]{:S(2)}) copy-start(bf16[512,128]{1,0:T(8,128)(2,1)S(1)} %fusion.34) | copy-start | bytes 393220
  274.5 71.5 %all-gather.9.cloned.1.call-start = ((), (), s32[]{:S(2)}) async-start(), calls=%async_computation.7 | async-start | bytes 5242880 | tf_op jit(solution)/shard_map/all_gather | solution.py:105
  285.6 142.6 %all-gather.13.cloned.1.call-start = ((), (), s32[]{:S(2)}) async-start(), calls=%async_computation.9 | async-start | bytes 5242880 | tf_op jit(solution)/shard_map/all_gather | solution.py:90
  286.2 261.1 %all-reduce.11.cloned.1.call-start = ((), (), s32[]{:S(2)}) async-start(), calls=%async_computation.10 | async-start | bytes 8388608 | tf_op jit(solution)/shard_map/psum | solution.py:134
  374.1 61.0 %copy-start.69 = (pred[2,1024]{1,0:T(4,128)(4,1)}, pred[2,1024]{1,0:T(4,128)(4,1)S(1)}, u32[]{:S(2)}) copy-start(pred[2,1024]{1,0:T(4,128)(4,1)S(1)} %get-tuple-element.541) | copy-start | bytes 6148
  374.1 61.0 %copy-start.73 = (f32[2,8,256]{2,1,0:T(8,128)}, f32[2,8,256]{2,1,0:T(8,128)S(1)}, u32[]{:S(2)}) copy-start(f32[2,8,256]{2,1,0:T(8,128)S(1)} %get-tuple-element.410) | copy-start | bytes 49156
  435.1 400.5 %all-gather.15.cloned.1.call-start = ((), (), s32[]{:S(2)}) async-start(), calls=%async_computation.11 | async-start | bytes 20971520 | tf_op jit(solution)/shard_map/all_gather | solution.py:143
  435.7 686.5 %all-gather.17.cloned.1.call-start = ((), (), s32[]{:S(2)}) async-start(), calls=%async_computation.12 | async-start | bytes 20971520 | tf_op jit(solution)/shard_map/all_gather | solution.py:144
  436.5 812.5 %all-reduce.13.cloned.1.call-start = ((), (), s32[]{:S(2)}) async-start(), calls=%async_computation.13 | async-start | bytes 8388608 | tf_op jit(solution)/shard_map/psum | solution.py:152
  458.6 91.9 %copy-start.47 = (bf16[512,128]{1,0:T(8,128)(2,1)}, bf16[512,128]{1,0:T(8,128)(2,1)S(1)}, u32[]{:S(2)}) copy-start(bf16[512,128]{1,0:T(8,128)(2,1)S(1)} %all-reduce.20) | copy-start | bytes 393220
  552.5 283.1 %copy-start.14 = (bf16[512,2048]{1,0:T(8,128)(2,1)}, bf16[512,2048]{1,0:T(8,128)(2,1)S(1)}, u32[]{:S(2)}) copy-start(bf16[512,2048]{1,0:T(8,128)(2,1)S(1)} %fusion.31) | copy-start | bytes 6291460
  1137.1 281.6 %all-reduce.17.cloned.1.call-start = ((), (), s32[]{:S(2)}) async-start(), calls=%async_computation.17 | async-start | bytes 8912896 | tf_op jit(solution)/shard_map/psum | solution.py:174
  1193.5 55.4 %copy-start.42 = (bf16[128,2048]{1,0:T(8,128)(2,1)S(1)}, bf16[128,2048]{1,0:T(8,128)(2,1)}, u32[]{:S(2)}) copy-start(bf16[128,2048]{1,0:T(8,128)(2,1)} %param.39) | copy-start | bytes 1572868
  1213.4 40.5 %copy-start.61 = (bf16[512,128]{1,0:T(8,128)(2,1)}, bf16[512,128]{1,0:T(8,128)(2,1)S(1)}, u32[]{:S(2)}) copy-start(bf16[512,128]{1,0:T(8,128)(2,1)S(1)} %all-reduce.21) | copy-start | bytes 393220
  1264.7 22.3 %copy-start.30 = (bf16[128,4096]{1,0:T(8,128)(2,1)S(1)}, bf16[128,4096]{1,0:T(8,128)(2,1)}, u32[]{:S(2)}) copy-start(bf16[128,4096]{1,0:T(8,128)(2,1)} %param.37) | copy-start | bytes 3145732
  1305.3 114.4 %copy-start.37 = (bf16[2048,128]{1,0:T(8,128)(2,1)S(1)}, bf16[2048,128]{1,0:T(8,128)(2,1)}, u32[]{:S(2)}) copy-start(bf16[2048,128]{1,0:T(8,128)(2,1)} %param.36) | copy-start | bytes 1572868
  1305.3 267.4 %reduce-scatter.3.cloned.1.call-start = ((), (), s32[]{:S(2)}) async-start(), calls=%async_computation.14 | async-start | bytes 5242880 | tf_op jit(solution)/shard_map/reduce_scatter | solution.py:227
  1528.1 91.7 %reduce-scatter.5.cloned.1.call-start = ((), (), s32[]{:S(2)}) async-start(), calls=%async_computation.15 | async-start | bytes 5242880 | tf_op jit(solution)/shard_map/reduce_scatter | solution.py:230
  1529.7 8.6 copy-start.24
  1533.2 185.6 %all-to-all-start.1 = ((bf16[2,256,2048]{2,0,1:T(2,128)(2,1)}), bf16[2,256,2048]{2,0,1:T(2,128)(2,1)}, u32[]{:S(2)}, u32[]{:S(2)}) async-start(bf16[2,256,2048]{2,0,1:T(2,128)(2,1)} %copy.68), calls=%async_computation.1 | async-start | bytes 4194304 | tf_op jit(solution)/shard_map/all_to_all | solution.py:279
  1537.9 167.4 %all-reduce.19.cloned.1.call-start = ((), (), s32[]{:S(2)}) async-start(), calls=%async_computation.18 | async-start | bytes 4980736 | tf_op jit(solution)/shard_map/psum | solution.py:252
  1633.4 360.0 %all-reduce.15.cloned.1.call-start = ((), (), s32[]{:S(2)}) async-start(), calls=%async_computation.16 | async-start | bytes 25165824 | tf_op jit(solution)/shard_map/psum | solution.py:263
  1645.5 59.7 %copy-start.72 = (f32[2,128]{1,0:T(2,128)S(1)}, f32[2,128]{1,0:T(2,128)}, u32[]{:S(2)}) copy-start(f32[2,128]{1,0:T(2,128)} %copy-done.71) | copy-start | bytes 3076
  1647.0 59.4 %copy-start.7 = (bf16[4,2,64,2048]{3,2,0,1:T(8,128)(2,1)S(1)}, bf16[4,2,64,2048]{3,2,0,1:T(8,128)(2,1)}, u32[]{:S(2)}) copy-start(bf16[4,2,64,2048]{3,2,0,1:T(8,128)(2,1)} %copy-done.6) | copy-start | bytes 6291460
  1718.7 76.3 %all-to-all-start.3 = ((bf16[2,256,2048]{2,0,1:T(2,128)(2,1)}), bf16[2,256,2048]{2,0,1:T(2,128)(2,1)S(1)}, u32[]{:S(2)}, u32[]{:S(2)}) async-start(bf16[2,256,2048]{2,0,1:T(2,128)(2,1)} %copy.76), calls=%async_computation.5 | async-start | bytes 4194304 | tf_op jit(solution)/shard_map/all_to_all | solution.py:280
  (76 other events, 260.5 us)
Sparse Core Ops, SparseCore 0:
  9.6 255.7 all-gather.6
  274.7 34.1 all-gather.10
  311.0 35.0 all-gather.8
  347.5 80.7 all-gather.12
  435.2 112.0 all-reduce.10
  548.8 286.7 all-gather.14
  837.2 284.9 all-gather.16
  1137.2 111.6 all-reduce.12
  1305.5 113.2 all-reduce.16
  1528.2 44.4 reduce-scatter.2
  1575.3 44.4 reduce-scatter.4
  1633.6 71.6 all-reduce.18
  1711.8 281.6 all-reduce.14
where the time goes:
time: 2020 us; the launch traced here: 2010 us
  waiting for transfers between devices  1520 us (75%)
  matrix products  235 us (12%)
  local copies, waits for them, and re-layouts  108 us (5%)
  blocking collectives  89.4 us (4%)
  other arithmetic  22 us (1%)
    all_gather x1, waiting for transfers between devices, local(): lax.all_gather(w_up, 'fsdp', axis=0, tiled=True)  276 us
    all_gather x1, waiting for transfers between devices, local(): lax.all_gather(w_down, 'fsdp', axis=1, tiled=True)  266 us
    psum x1, waiting for transfers between devices, local(): lax.psum((grad_a_qkv, grad_b_qkv, grad_a_out, grad_b_out, grad_a_up, grad...  196 us
    all_gather x1, waiting for transfers between devices, local(): lax.all_gather(w_qkv, 'fsdp', axis=1, tiled=True)  141 us
    psum x1, waiting for transfers between devices, local(): lax.psum((part_hidden, part_adapt_up), 'tp')  113 us
    all_to_all x1, waiting for transfers between devices, local(): lax.all_to_all(x_in, 'fsdp', split_axis=0, concat_axis=1, tiled=True)  104 us
    psum x1, waiting for transfers between devices, local(): attn_sum, adapt_out_sum = lax.psum((part_out, part_adapt), 'tp')  88.7 us
    dot_general x18, matrix products, product(): return jnp.dot(left_side, right_side, preferred_element_type=jnp.float32)  86.5 us
  transfers between devices with their start and end apart: 16, of which 15 were waited for; matrix products, arithmetic and copies ran while one was open for 7% of the time, Pallas kernels for 0%

commit v1 on v0

--- a/solution.py
+++ b/solution.py
@@ -60,6 +60,21 @@
     a_down,
     b_down,
 ):
+
+    def refer_skins_on_mesh(vec, along_dim):
+        current_block = lax.psum(1, "fsdp")
+        known = lax.axis_index("fsdp")
+        e_next, s_next = (current_block, known)
+        aux, piece_out = (vec, 1)
+        while piece_out < e_next:
+            then = tuple(((t, t ^ piece_out) for t in range(e_next)))
+            w1 = lax.ppermute(aux, "fsdp", perm=then)
+            big = jnp.concatenate([aux, w1], along_dim)
+            tile_out = jnp.concatenate([w1, aux], along_dim)
+            aux = jnp.where(s_next & piece_out == 0, big, tile_out)
+            piece_out = 2 * piece_out
+        return aux
+
     n_ctx = lax.axis_size("ctx")
     n_fsdp = lax.axis_size("fsdp")
     owner_index = lax.axis_index("fsdp")
@@ -140,7 +155,7 @@
     )
     hidden_low = hidden_one.astype(jnp.bfloat16)
     up_full, down_full = (
-        lax.all_gather(w_up, "fsdp", axis=0, tiled=True),
+        refer_skins_on_mesh(w_up, along_dim=0),
         lax.all_gather(w_down, "fsdp", axis=1, tiled=True),
     )
     adapt_up = (product(hidden_low, a_up) * pick_rows).astype(jnp.bfloat16)

time: 2020 us -> 2330 us (1.15)
  waiting for transfers between devices: 1520 us -> 1840 us
    ppermute x0 -> x2, waiting for transfers between devices: none -> 700 us  [refer_skins_on_mesh(): w1 = lax.ppermute(aux, 'fsdp', perm=then)]
    all_gather x1, waiting for transfers between devices: 266 us -> 0.01 us  [local(): lax.all_gather(w_down, 'fsdp', axis=1, tiled=True)]
    psum x1, waiting for transfers between devices: 88.7 us -> 0.02 us  [local(): attn_sum, adapt_out_sum = lax.psum((part_out, part_adapt), 'tp')]
    all_gather x1, waiting for transfers between devices: 276 us -> 244 us  [local(): lax.all_gather(w_up, 'fsdp', axis=0, tiled=True)]
  transfers between devices with their start and end apart: 16 -> 18, of which waited for: 15 -> 15; matrix products, arithmetic and copies ran while one was open for 7% -> 9% of each run, Pallas kernels for 0% -> 0%
where the time goes in v1:
time: 2330 us
  waiting for transfers between devices  1840 us (79%)
  matrix products  233 us (10%)
  local copies, waits for them, and re-layouts  108 us (5%)
  blocking collectives  83.2 us (4%)
  other arithmetic  33.2 us (1%)
    ppermute x2, waiting for transfers between devices, refer_skins_on_mesh(): w1 = lax.ppermute(aux, 'fsdp', perm=then)  700 us
    all_gather x1, waiting for transfers between devices, local(): lax.all_gather(w_up, 'fsdp', axis=0, tiled=True)  244 us
    psum x1, waiting for transfers between devices, local(): lax.psum((grad_a_qkv, grad_b_qkv, grad_a_out, grad_b_out, grad_a_up, grad...  196 us
    all_gather x1, waiting for transfers between devices, local(): lax.all_gather(w_qkv, 'fsdp', axis=1, tiled=True)  141 us
    psum x1, waiting for transfers between devices, local(): lax.psum((part_hidden, part_adapt_up), 'tp')  112 us
    all_to_all x1, waiting for transfers between devices, local(): lax.all_to_all(x_in, 'fsdp', split_axis=0, concat_axis=1, tiled=True)  104 us
    dot_general x18, matrix products, against(): lax.dot_general(left_side, right_side, (((1,), (1,)), ((), ())), preferre...  83.5 us
    dot_general x18, matrix products, product(): return jnp.dot(left_side, right_side, preferred_element_type=jnp.float32)  81.9 us
  transfers between devices with their start and end apart: 18, of which 15 were waited for; matrix products, arithmetic and copies ran while one was open for 9% of the time, Pallas kernels for 0%

profile of v1, /device:TPU:0, one launch (start us, length us, event | category | flops | bytes accessed | tf_op | source)
XLA Modules:
  0.0 2326.2 jit_solution(11973201563506646407)
XLA Ops:
  7.9 6.3 all-to-all-start
  14.6 104.2 %all-to-all-done = bf16[8,64,2048]{2,1,0:T(8,128)(2,1)S(1)} async-done(((bf16[8,64,2048]{2,1,0:T(8,128)(2,1)}), bf16[8,64,2048]{2,1,0:T(8,128)(2,1)S(1)}, u32[]{:S(2)}, u32[]{:S(2)}) %all-to-all-start) | async-done | bytes 2097184 | tf_op jit(solution)/shard_map/all_to_all | solution.py:90
  124.0 141.4 %all-gather.7.cloned.1.call-done = bf16[3,2048,1024]{2,1,0:T(8,128)(2,1)} async-done(((bf16[3,512,1024]{2,1,0:T(8,128)(2,1)}), bf16[3,2048,1024]{2,1,0:T(8,128)(2,1)}) %all-gather.7.cloned.1.call-update) | async-done | bytes 12582928 | tf_op jit(solution)/shard_map/all_gather | solution.py:104
  297.6 11.3 all-gather.11.cloned.1.call-done
  308.8 37.2 %all-gather.9.cloned.1.call-done = bf16[2,1024,1024]{1,2,0:T(8,128)(2,1)} async-done(((bf16[2,256,1024]{1,2,0:T(8,128)(2,1)}), bf16[2,1024,1024]{1,2,0:T(8,128)(2,1)}) %all-gather.9.cloned.1.call-update) | async-done | bytes 4194320 | tf_op jit(solution)/shard_map/all_gather | solution.py:120
  347.1 26.9 %while.26 = (s32[]{:T(128)}, bf16[2,256,1024]{2,1,0:T(8,128)(2,1)}, f32[2,8,256]{2,1,0:T(8,128)S(1)}, bf16[2,1024,1024]{1,2,0:T(8,128)(2,1)}, pred[2,1024]{1,0:T...) while((s32[]{:T(128)}, bf16[2,256,1024]{2,1,0:T(8,128)(2,1)}, ...), condition=%wide.region_3.4_spmd, body=%wide.region_0.3_spmd.sunk | while | flops 1097070592 | bytes 46208640 | solution.py:145
  374.1 54.2 %all-gather.13.cloned.1.call-done = bf16[1024,2048]{1,0:T(8,128)(2,1)} async-done(((bf16[1024,512]{1,0:T(8,128)(2,1)}), bf16[1024,2048]{1,0:T(8,128)(2,1)}) %all-gather.13.cloned.1.call-update) | async-done | bytes 4194320 | tf_op jit(solution)/shard_map/all_gather | solution.py:105
  428.3 6.8 fusion.110
  435.8 92.6 %collective-permute-done = bf16[512,4096]{1,0:T(8,128)(2,1)} collective-permute-done((bf16[512,4096]{1,0:T(8,128)(2,1)}, bf16[512,4096]{1,0:T(8,128)(2,1)}, u32[]{:S(2)}, u32[]{:S(2)}) %collective-permute-start) | collective-permute-done | bytes 4194336 | tf_op jit(solution)/shard_map/ppermute | solution.py:71
  528.4 11.2 maximum_select_fusion.2
  542.9 13.3 all-reduce.20
  564.3 607.3 %collective-permute-done.1 = bf16[1024,4096]{1,0:T(8,128)(2,1)} collective-permute-done((bf16[1024,4096]{1,0:T(8,128)(2,1)}, bf16[1024,4096]{1,0:T(8,128)(2,1)}, u32[]{:S(2)}, u32[]{:S(2)}) %collective-permute-start.1) | collective-permute-done | bytes 8388640 | tf_op jit(solution)/shard_map/ppermute | solution.py:71
  1171.6 19.7 multiply_convert_fusion.1
  1191.3 15.0 fusion.112
  1207.9 51.1 %all_to_all.60 = bf16[8,64,2048]{2,1,0:T(8,128)(2,1)S(1)} all-to-all(bf16[8,64,2048]{2,1,0:T(8,128)(2,1)S(1)} %copy-done.38), channel_id=1, replica_groups=mesh['fsdp'=4,'ctx'=4,'tp'=2] {'fsdp'}, dimensions={0} | all-to-all | bytes 4194304 | tf_op jit(solution)/shard_map/all_to_all | solution.py:91
  1263.9 18.8 all-reduce.21
  1282.7 35.3 %all-reduce.13.cloned.1.call-done = f32[512,2048]{1,0:T(8,128)} async-done(((f32[512,2048]{1,0:T(8,128)}), f32[512,2048]{1,0:T(8,128)}) %all-reduce.13.cloned.1.call-update) | async-done | bytes 4194320 | tf_op jit(solution)/shard_map/psum | solution.py:167
  1334.4 23.2 fusion.29
  1361.8 244.0 %all-gather.17.cloned.1.call-done = bf16[2048,4096]{1,0:T(8,128)(2,1)} async-done(((bf16[512,4096]{1,0:T(8,128)(2,1)}), bf16[2048,4096]{1,0:T(8,128)(2,1)}) %all-gather.17.cloned.1.call-update) | async-done | bytes 16777232 | tf_op jit(solution)/shard_map/all_gather | solution.py:177
  1605.8 15.5 fusion.114
  1621.4 112.2 %all-reduce.17.cloned.1.call-done = (f32[512,2048]{1,0:T(8,128)}, f32[512,128]{1,0:T(8,128)}) async-done(((f32[512,2048]{1,0:T(8,128)}, f32[512,128]{1,0:T(8,128)}), (f32[512,2048]{1,0:T(8,128)}, f32[512,128]{1,0:T(8,128)})) %all-reduce.17.cloned.1.call-update) | async-done | bytes 4456464 | tf_op jit(solution)/shard_map/psum | solution.py:189
  1751.3 91.5 %while.27 = (s32[]{:T(128)}, bf16[2,256,1024]{2,1,0:T(8,128)(2,1)}, bf16[2,1024,1024]{2,1,0:T(8,128)(2,1)}, bf16[2,1024,1024]{2,1,0:T(8,128)(2,1)}, bf16[2,1024,...) while((s32[]{:T(128)}, bf16[2,256,1024]{2,1,0:T(8,128)(2,1)}, ...), condition=%wide.region_20.21_spmd, body=%wide.region_18.20_spmd.sunk | while | flops 2718431232 | bytes 173603120 | solution.py:238
  1762.0 6.4 multiply_reduce_fusion.6
  1778.9 6.8 fusion.241
  1807.5 6.4 multiply_reduce_fusion.6
  1824.4 6.8 fusion.241
  1853.4 6.8 fusion.35
  1860.2 27.3 %reduce-scatter.3.cloned.1.call-done = bf16[2,256,1024]{2,1,0:T(8,128)(2,1)} async-done(((bf16[2,1024,1024]{2,1,0:T(8,128)(2,1)}), bf16[2,256,1024]{2,1,0:T(8,128)(2,1)}) %reduce-scatter.3.cloned.1.call-update) | async-done | bytes 1048592 | tf_op jit(solution)/shard_map/reduce_scatter | solution.py:242
  1889.1 45.4 %reduce-scatter.5.cloned.1.call-done = bf16[2,256,1024]{2,1,0:T(8,128)(2,1)} async-done(((bf16[2,1024,1024]{2,1,0:T(8,128)(2,1)}), bf16[2,256,1024]{2,1,0:T(8,128)(2,1)}) %reduce-scatter.5.cloned.1.call-update) | async-done | bytes 1048592 | tf_op jit(solution)/shard_map/reduce_scatter | solution.py:245
  1963.7 56.3 %all-reduce.19.cloned.1.call-done = (bf16[3,512,128]{2,1,0:T(8,128)(2,1)}, bf16[512,2048]{1,0:T(8,128)(2,1)}) async-done(((bf16[3,512,128]{2,1,0:T(8,128)(2,1)}, bf16[512,2048]{1,0:T(8,128)(2,1)}), (bf16[3,512,128]{2,1,0:T(8,128)(2,1)}, bf16[512,2048]{1,0:T(8,128)(2,1)})) %all-reduce.19.cloned.1.call-update) | async-done | bytes 2490384 | tf_op jit(solution)/shard_map/psum | solution.py:267
  2041.9 67.8 %all-to-all-done.3 = bf16[2,256,2048]{2,0,1:T(2,128)(2,1)S(1)} async-done(((bf16[2,256,2048]{2,0,1:T(2,128)(2,1)}), bf16[2,256,2048]{2,0,1:T(2,128)(2,1)S(1)}, u32[]{:S(2)}, u32[]{:S(2)}) %all-to-all-start.3) | async-done | bytes 2097184 | tf_op jit(solution)/shard_map/all_to_all | solution.py:295
  2112.0 196.2 %all-reduce.15.cloned.1.call-done = (f32[3,2048,128]{1,2,0:T(8,128)}, f32[3,128,1024]{2,1,0:T(8,128)}, f32[1024,128]{1,0:T(8,128)}, f32[128,2048]{1,0:T(8,128)},...) async-done(((f32[3,2048,128]{1,2,0:T(8,128)}, f32[3,128,1024]{2,1,0:T(8,128)}, f32[1024,128]{1,0:T(8,128)}, ...) | async-done | bytes 12582928 | tf_op jit(solution)/shard_map/psum | solution.py:278
  (364 shorter events, 263.9 us)
Async XLA Ops:
  7.2 1254.4 %copy-start = (bf16[4096,128]{1,0:T(8,128)(2,1)S(1)}, bf16[4096,128]{1,0:T(8,128)(2,1)}, u32[]{:S(2)}) copy-start(bf16[4096,128]{1,0:T(8,128)(2,1)} %param.38) | copy-start | bytes 3145732
  7.2 258.2 %all-gather.7.cloned.1.call-start = ((), (), s32[]{:S(2)}) async-start(), calls=%async_computation.6 | async-start | bytes 15728640 | tf_op jit(solution)/shard_map/all_gather | solution.py:104
  7.9 110.8 %all-to-all-start = ((bf16[8,64,2048]{2,1,0:T(8,128)(2,1)}), bf16[8,64,2048]{2,1,0:T(8,128)(2,1)S(1)}, u32[]{:S(2)}, u32[]{:S(2)}) async-start(bf16[8,64,2048]{2,1,0:T(8,128)(2,1)} %param.22), calls=%async_computation | async-start | bytes 4194304 | tf_op jit(solution)/shard_map/all_to_all | solution.py:90
  14.3 294.6 %all-gather.11.cloned.1.call-start = ((), (), s32[]{:S(2)}) async-start(), calls=%async_computation.8 | async-start | bytes 5242880 | tf_op jit(solution)/shard_map/all_gather | solution.py:119
  14.6 1728.1 %copy-start.70 = (f32[2,128]{1,0:T(2,128)}, f32[2,128]{1,0:T(2,128)S(1)}, u32[]{:S(2)}) copy-start(f32[2,128]{1,0:T(2,128)S(1)} %reshape.257) | copy-start | bytes 3076
  121.8 434.5 %copy-start.6 = (bf16[4,2,64,2048]{3,2,0,1:T(8,128)(2,1)}, bf16[4,2,64,2048]{3,2,0,1:T(8,128)(2,1)S(1)}, u32[]{:S(2)}) copy-start(bf16[4,2,64,2048]{3,2,0,1:T(8,128)(2,1)S(1)} %copy.63) | copy-start | bytes 6291460
  124.0 145.9 %copy-start.52 = (bf16[512,128]{1,0:T(8,128)(2,1)}, bf16[512,128]{1,0:T(8,128)(2,1)S(1)}, u32[]{:S(2)}) copy-start(bf16[512,128]{1,0:T(8,128)(2,1)S(1)} %fusion.42) | copy-start | bytes 393220
  274.5 71.5 %all-gather.9.cloned.1.call-start = ((), (), s32[]{:S(2)}) async-start(), calls=%async_computation.7 | async-start | bytes 5242880 | tf_op jit(solution)/shard_map/all_gather | solution.py:120
  285.6 142.6 %all-gather.13.cloned.1.call-start = ((), (), s32[]{:S(2)}) async-start(), calls=%async_computation.9 | async-start | bytes 5242880 | tf_op jit(solution)/shard_map/all_gather | solution.py:105
  286.2 270.1 %all-reduce.11.cloned.1.call-start = ((), (), s32[]{:S(2)}) async-start(), calls=%async_computation.10 | async-start | bytes 8388608 | tf_op jit(solution)/shard_map/psum | solution.py:149
  374.1 61.0 %copy-start.68 = (pred[2,1024]{1,0:T(4,128)(4,1)}, pred[2,1024]{1,0:T(4,128)(4,1)S(1)}, u32[]{:S(2)}) copy-start(pred[2,1024]{1,0:T(4,128)(4,1)S(1)} %get-tuple-element.542) | copy-start | bytes 6148
  374.1 61.0 %copy-start.72 = (f32[2,8,256]{2,1,0:T(8,128)}, f32[2,8,256]{2,1,0:T(8,128)S(1)}, u32[]{:S(2)}) copy-start(f32[2,8,256]{2,1,0:T(8,128)S(1)} %get-tuple-element.410) | copy-start | bytes 49156
  435.1 756.2 %all-gather.15.cloned.1.call-start = ((), (), s32[]{:S(2)}) async-start(), calls=%async_computation.11 | async-start | bytes 20971520 | tf_op jit(solution)/shard_map/all_gather | solution.py:159
  435.7 882.4 %all-reduce.13.cloned.1.call-start = ((), (), s32[]{:S(2)}) async-start(), calls=%async_computation.12 | async-start | bytes 8388608 | tf_op jit(solution)/shard_map/psum | solution.py:167
  435.7 92.7 %collective-permute-start = (bf16[512,4096]{1,0:T(8,128)(2,1)}, bf16[512,4096]{1,0:T(8,128)(2,1)}, u32[]{:S(2)}, u32[]{:S(2)}) collective-permute-start(bf16[512,4096]{1,0:T(8,128)(2,1)} %param.28), channel_id=1, source_target_pairs={{0,8},{8,0},{16,24},{24,16},{1,9},{9,1},{17,25},{25,17},{2,10},{10... | collective-permute-start | bytes 12582920 | tf_op jit(solution)/shard_map/ppermute | solution.py:71
  435.8 104.7 %copy-start.78 = (f32[2,2048]{1,0:T(2,128)S(1)}, f32[2,2048]{1,0:T(2,128)}, u32[]{:S(2)}) copy-start(f32[2,2048]{1,0:T(2,128)} %param.30) | copy-start | bytes 49156
  435.8 104.7 %copy-start.79 = (f32[2,2048]{1,0:T(2,128)S(1)}, f32[2,2048]{1,0:T(2,128)}, u32[]{:S(2)}) copy-start(f32[2,2048]{1,0:T(2,128)} %param.31) | copy-start | bytes 49156
  435.8 104.7 %copy-start.65 = (bf16[1024,128]{1,0:T(8,128)(2,1)S(1)}, bf16[1024,128]{1,0:T(8,128)(2,1)}, u32[]{:S(2)}) copy-start(bf16[1024,128]{1,0:T(8,128)(2,1)} %param.34) | copy-start | bytes 786436
  539.6 632.0 %collective-permute-start.1 = (bf16[1024,4096]{1,0:T(8,128)(2,1)}, bf16[1024,4096]{1,0:T(8,128)(2,1)}, u32[]{:S(2)}, u32[]{:S(2)}) collective-permute-start(bf16[1024,4096]{1,0:T(8,128)(2,1)} %maximum_select_fusion.2), channel_id=1, source_target_pairs={{0,16},{8,24},{16,0},{24,8},{1,17},{9,25},{17,1},{25,9},{2,18},{10... | collective-permute-start | bytes 25165832 | tf_op jit(solution)/shard_map/ppermute | solution.py:71
  562.0 609.6 %copy-start.14 = (bf16[512,2048]{1,0:T(8,128)(2,1)}, bf16[512,2048]{1,0:T(8,128)(2,1)S(1)}, u32[]{:S(2)}) copy-start(bf16[512,2048]{1,0:T(8,128)(2,1)S(1)} %fusion.39) | copy-start | bytes 6291460
  1206.3 399.5 %all-gather.17.cloned.1.call-start = ((), (), s32[]{:S(2)}) async-start(), calls=%async_computation.13 | async-start | bytes 20971520 | tf_op jit(solution)/shard_map/all_gather | solution.py:177
  1207.1 526.5 %all-reduce.17.cloned.1.call-start = ((), (), s32[]{:S(2)}) async-start(), calls=%async_computation.17 | async-start | bytes 8912896 | tf_op jit(solution)/shard_map/psum | solution.py:189
  1262.6 55.4 %copy-start.41 = (bf16[128,2048]{1,0:T(8,128)(2,1)S(1)}, bf16[128,2048]{1,0:T(8,128)(2,1)}, u32[]{:S(2)}) copy-start(bf16[128,2048]{1,0:T(8,128)(2,1)} %param.39) | copy-start | bytes 1572868
  1621.3 113.2 %copy-start.36 = (bf16[2048,128]{1,0:T(8,128)(2,1)S(1)}, bf16[2048,128]{1,0:T(8,128)(2,1)}, u32[]{:S(2)}) copy-start(bf16[2048,128]{1,0:T(8,128)(2,1)} %param.36) | copy-start | bytes 1572868
  1621.4 266.1 %reduce-scatter.3.cloned.1.call-start = ((), (), s32[]{:S(2)}) async-start(), calls=%async_computation.14 | async-start | bytes 5242880 | tf_op jit(solution)/shard_map/reduce_scatter | solution.py:242
  1842.8 91.8 %reduce-scatter.5.cloned.1.call-start = ((), (), s32[]{:S(2)}) async-start(), calls=%async_computation.15 | async-start | bytes 5242880 | tf_op jit(solution)/shard_map/reduce_scatter | solution.py:245
  1847.8 185.7 %all-to-all-start.1 = ((bf16[2,256,2048]{2,0,1:T(2,128)(2,1)}), bf16[2,256,2048]{2,0,1:T(2,128)(2,1)}, u32[]{:S(2)}, u32[]{:S(2)}) async-start(bf16[2,256,2048]{2,0,1:T(2,128)(2,1)} %copy.68), calls=%async_computation.1 | async-start | bytes 4194304 | tf_op jit(solution)/shard_map/all_to_all | solution.py:294
  1852.5 167.5 %all-reduce.19.cloned.1.call-start = ((), (), s32[]{:S(2)}) async-start(), calls=%async_computation.18 | async-start | bytes 4980736 | tf_op jit(solution)/shard_map/psum | solution.py:267
  1948.2 360.0 %all-reduce.15.cloned.1.call-start = ((), (), s32[]{:S(2)}) async-start(), calls=%async_computation.16 | async-start | bytes 25165824 | tf_op jit(solution)/shard_map/psum | solution.py:278
  1960.3 59.8 %copy-start.71 = (f32[2,128]{1,0:T(2,128)S(1)}, f32[2,128]{1,0:T(2,128)}, u32[]{:S(2)}) copy-start(f32[2,128]{1,0:T(2,128)} %copy-done.70) | copy-start | bytes 3076
  1961.7 59.4 %copy-start.7 = (bf16[4,2,64,2048]{3,2,0,1:T(8,128)(2,1)S(1)}, bf16[4,2,64,2048]{3,2,0,1:T(8,128)(2,1)}, u32[]{:S(2)}) copy-start(bf16[4,2,64,2048]{3,2,0,1:T(8,128)(2,1)} %copy-done.6) | copy-start | bytes 6291460
  2033.5 76.3 %all-to-all-start.3 = ((bf16[2,256,2048]{2,0,1:T(2,128)(2,1)}), bf16[2,256,2048]{2,0,1:T(2,128)(2,1)S(1)}, u32[]{:S(2)}, u32[]{:S(2)}) async-start(bf16[2,256,2048]{2,0,1:T(2,128)(2,1)} %copy.76), calls=%async_computation.5 | async-start | bytes 4194304 | tf_op jit(solution)/shard_map/all_to_all | solution.py:295
  (79 other events, 344.4 us)
Sparse Core Ops, SparseCore 0:
  9.6 255.7 all-gather.6
  274.7 34.1 all-gather.10
  311.0 35.0 all-gather.8
  347.5 80.7 all-gather.12
  435.2 106.3 all-reduce.10
  543.1 583.8 all-gather.14
  1206.4 111.5 all-reduce.12
  1319.6 286.1 all-gather.16
  1621.5 112.0 all-reduce.16
  1842.9 44.5 reduce-scatter.2
  1890.0 44.5 reduce-scatter.4
  1948.3 71.6 all-reduce.18
  2026.5 281.6 all-reduce.14
